TPU v7x, 32 devices: a whole 2x2x4 slice. The times are simulated.
32 devices in a mesh: band: 4 (over y, core), lev: 8 (over z, x).
Axes of the slice: x: 2, y: 2, z: 4, core: 2. Of those that a mesh axis runs over, the one named last changes fastest.
Arguments:
- azimuthal_coeffs: bfloat16 [2560, 64, 64], P('band', 'lev'), may hold values from -6 to 6
- polynomial_tables: bfloat16 [32, 2, 448, 1280], P(('band', 'lev')), may hold values from -0.15625 to 0.15625
- gauss_masses: float32 [1280], replicated, may hold values from 0.3 to 1.5
- circle_samples: int32 [1280], replicated, may hold values from 20 to 152, as said below
- table_lookup: int32 [32], replicated, may hold values from 0 to 31, each once
- eigen_basis: float32 [16, 16], replicated, may hold values from -1.5 to 1.5
- basis_mapping: float32 [16, 16], replicated, may hold values from -1.5 to 1.5
- eigen_constants: float32 [16], replicated, may hold values from 0.5 to 2
- hydrostatic_matrix: float32 [16, 16], replicated, may hold values from -1.5 to 1.5
- thermal_response: float32 [16, 16], replicated, may hold values from -1.5 to 1.5
Outputs:
- advanced: bfloat16 [2560, 64, 64], P('band', 'lev')
Inputs may be any that keep to these rules, and one draw needn't show every extreme that they name: circle_samples[j] is 20 + 4 * floor(j * 32 / 1280) plus 0, 4 or 8; row 0 holds 20 and row 1279 the largest value. table_lookup is a permutation of 0 .. 31.
All inputs are finite; a program needn't handle non-finite values.
Results may differ from a plain program's by a relative error of at most 0.0041.
The roundings to bfloat16 on the way count: a program that leaves them out, or rounds other values in their place, can miss the bound.
Values may be sent and summed in bfloat16 or wider, within the bound.
No kernel may reach another device: no remote copies, remote signals or barrier semaphores. Data moves between devices by JAX's collectives and lax.ppermute only.
A program may use at most 64 MiB of HBM per device.

v0:
```python
import jax
import jax.numpy as jnp
from jax import lax
from jax.sharding import PartitionSpec as P

TRUNC = 1280
FIELDS = 4
TRUNCATION_LIMIT = lax.Precision.HIGHEST
STIFFNESS = 8.0
DIFFUSION = 4.0


def harmonic_advance(
    harmonic_current,
    total_order,
    eigen_basis,
    basis_mapping,
    eigen_constants,
    hydrostatic_matrix,
    thermal_response,
):
    scaled = total_order * (total_order + 1.0) / (TRUNC * (TRUNC + 1.0))
    implicit_weighting = STIFFNESS * scaled
    rotational_curl = harmonic_current[:, 0]
    dilatation_current = harmonic_current[:, 1]
    thermal_current = harmonic_current[:, 2]
    moisture = harmonic_current[:, 3]
    hyper_viscosity = 1.0 / (1.0 + DIFFUSION * scaled * scaled)
    explicit_righthand = dilatation_current + implicit_weighting[:, None, None] * jnp.einsum(
        "li,eic->elc", hydrostatic_matrix, thermal_current, precision=TRUNCATION_LIMIT
    )
    projected = jnp.einsum(
        "li,eic->elc", basis_mapping, explicit_righthand, precision=TRUNCATION_LIMIT
    )
    projected = projected / (
        1.0 + implicit_weighting[:, None, None] * eigen_constants[None, :, None]
    )
    dilatation_future = jnp.einsum(
        "li,eic->elc", eigen_basis, projected, precision=TRUNCATION_LIMIT
    )
    thermal_future = thermal_current - jnp.einsum(
        "li,eic->elc", thermal_response, dilatation_future, precision=TRUNCATION_LIMIT
    )
    return jnp.stack(
        [
            rotational_curl * hyper_viscosity[:, None, None],
            dilatation_future,
            thermal_future,
            moisture * hyper_viscosity[:, None, None],
        ],
        axis=1,
    )


def analyse_wave(column, zonal_order, operator_array, gauss_masses, circle_samples):
    half_rows = operator_array.shape[2]
    live_mask = (2 * zonal_order < circle_samples).astype(jnp.float32)
    north = column[:half_rows].astype(jnp.float32)
    south = jnp.flip(column[half_rows:], axis=0).astype(jnp.float32)
    weight_col = (gauss_masses * live_mask)[:, None]
    even_part = ((north + south) * weight_col).astype(jnp.bfloat16)
    odd_part = ((north - south) * weight_col).astype(jnp.bfloat16)
    spec_even = jnp.dot(operator_array[0], even_part, preferred_element_type=jnp.float32)
    spec_odd = jnp.dot(operator_array[1], odd_part, preferred_element_type=jnp.float32)
    return jnp.stack([spec_even, spec_odd], axis=0)


def complete_harmonic(
    harmonic_coeffs,
    zonal_order,
    operator_array,
    circle_samples,
    eigen_basis,
    basis_mapping,
    eigen_constants,
    hydrostatic_matrix,
    thermal_response,
):
    pair_rows = harmonic_coeffs.shape[1]
    col_count = harmonic_coeffs.shape[2]
    offsets = jnp.arange(pair_rows, dtype=jnp.int32) * 2 + zonal_order
    keep_even = (offsets < TRUNC).astype(jnp.float32)[:, None]
    keep_odd = (offsets + 1 < TRUNC).astype(jnp.float32)[:, None]
    harmonic_current = jnp.concatenate(
        [harmonic_coeffs[0] * keep_even, harmonic_coeffs[1] * keep_odd], axis=0
    )
    total_order = jnp.concatenate([offsets, offsets + 1]).astype(jnp.float32)
    arranged = harmonic_current.reshape(2 * pair_rows, FIELDS, col_count // (2 * FIELDS), 2)
    refreshed = harmonic_advance(
        arranged,
        total_order,
        eigen_basis,
        basis_mapping,
        eigen_constants,
        hydrostatic_matrix,
        thermal_response,
    )
    refreshed = refreshed.reshape(2 * pair_rows, col_count).astype(jnp.bfloat16)
    contract = (((0,), (0,)), ((), ()))
    even_sum = lax.dot_general(
        operator_array[0], refreshed[:pair_rows], contract, preferred_element_type=jnp.float32
    )
    odd_sum = lax.dot_general(
        operator_array[1], refreshed[pair_rows:], contract, preferred_element_type=jnp.float32
    )
    live_col = (2 * zonal_order < circle_samples).astype(jnp.float32)[:, None]
    north_out = (even_sum + odd_sum) * live_col
    south_out = (even_sum - odd_sum) * live_col
    return jnp.concatenate([north_out, jnp.flip(south_out, axis=0)], axis=0).astype(jnp.bfloat16)


def per_device(
    azimuthal_coeffs,
    polynomial_tables,
    gauss_masses,
    circle_samples,
    table_lookup,
    eigen_basis,
    basis_mapping,
    eigen_constants,
    hydrostatic_matrix,
    thermal_response,
):
    lat_rows, level_cols, last_width = azimuthal_coeffs.shape
    wave_count = last_width // 2
    band_count = lax.axis_size("band")
    lev_count = lax.axis_size("lev")
    device_id = lax.axis_index("band") * lev_count + lax.axis_index("lev")
    serial = jnp.arange(wave_count, dtype=jnp.int32)
    wave_of = jnp.zeros((wave_count,), jnp.int32).at[table_lookup].set(serial)
    own_wave = jnp.sum(jnp.where(table_lookup == device_id, serial, 0))
    operator_array = polynomial_tables[0]
    parts = jnp.arange(2, dtype=jnp.int32)[None, :]
    column_pick = (2 * wave_of[:, None] + parts).reshape(-1)
    ordered = jnp.take(azimuthal_coeffs, column_pick, axis=2)
    ordered = ordered.reshape(lat_rows, level_cols, band_count, lev_count, 2)
    ordered = jnp.transpose(ordered, (0, 2, 3, 1, 4)).reshape(
        lat_rows, band_count, lev_count * level_cols * 2
    )
    level_mixed = lax.all_to_all(ordered, "lev", split_axis=2, concat_axis=2, tiled=True)
    harmonic_coeffs = analyse_wave(
        lax.all_to_all(level_mixed, "band", split_axis=1, concat_axis=0, tiled=True)[:, 0, :],
        own_wave,
        operator_array,
        gauss_masses,
        circle_samples,
    )
    result = complete_harmonic(
        harmonic_coeffs,
        own_wave,
        operator_array,
        circle_samples,
        eigen_basis,
        basis_mapping,
        eigen_constants,
        hydrostatic_matrix,
        thermal_response,
    )
    returned = lax.all_to_all(
        lax.all_to_all(result[:, None, :], "band", split_axis=0, concat_axis=1, tiled=True),
        "lev",
        split_axis=2,
        concat_axis=2,
        tiled=True,
    )
    returned = returned.reshape(lat_rows, band_count, lev_count, level_cols, 2)
    returned = jnp.transpose(returned, (0, 3, 1, 2, 4)).reshape(lat_rows, level_cols, last_width)
    back_pick = (2 * table_lookup[:, None] + parts).reshape(-1)
    return jnp.take(returned, back_pick, axis=2)


def solution(mesh):
    placed = (
        P("band", "lev", None),
        P(("band", "lev"), None, None, None),
        P(),
        P(),
        P(),
        P(),
        P(),
        P(),
        P(),
        P(),
    )
    return jax.shard_map(
        per_device, mesh=mesh, in_specs=placed, out_specs=P("band", "lev", None), check_vma=False
    )
```

profile of v0, /device:TPU:0, one launch (start us, length us, event | category | flops | bytes accessed | tf_op | source)
XLA Modules:
  0.0 95.0 jit_solution(13781600453538992396)
XLA Ops:
  0.0 0.0 copy-start
  0.0 1.4 %broadcast_multiply_fusion = (s32[32]{0:T(128)S(1)}, s32[32]{0:T(128)S(1)}, s32[]{:T(128)}) fusion(s32[32]{0:T(128)} %param.16, s32[]{:T(128)S(6)} %add.120), kind=kLoop, calls=%fused_computation.77 | loop fusion | flops 223 | bytes 392 | tf_op jit(solution)/shard_map/mul | solution.py:168
  1.4 0.7 scatter_custom_fusion
  2.1 0.1 iota_add_fusion.1
  2.1 0.1 add.118
  2.3 2.5 %gather_fusion = bf16[64,640,8]{1,0,2:T(8,128)(2,1)S(1)} fusion(bf16[640,8,64]{0,2,1:T(8,128)(2,1)S(1)} %copy-done, s32[1024]{0:T(1024)S(1)} %pad_clamp_fusion.1), kind=kCustom, calls=%fused_computation.clone | custom fusion | bytes 1310976 | tf_op jit(solution)/shard_map/jit(_take)/gather | solution.py:135
  4.9 0.1 select_bitcast_fusion.1
  5.0 0.2 reshape.147
  5.3 0.0 copy-start.4
  5.3 1.1 %copy.64 = bf16[640,8,4,8,2]{0,2,4,1,3:T(4,128)(2,1)} copy(bf16[640,8,4,8,2]{0,4,3,2,1:T(2,128)(2,1)S(1)} %reshape.147) | data formatting | bytes 1310720 | tf_op jit(solution)/shard_map/reshape | solution.py:136
  6.4 7.3 %all-to-all-start = ((bf16[640,4,128]{0,1,2:T(4,128)(2,1)}), bf16[640,4,128]{0,1,2:T(4,128)(2,1)S(1)}, u32[]{:S(2)}, u32[]{:S(2)}) async-start(bf16[640,4,128]{0,1,2:T(4,128)(2,1)} %bitcast.2), calls=%async_computation | async-start | bytes 1310720 | tf_op jit(solution)/shard_map/all_to_all | solution.py:140
  14.3 0.6 multiply_add_fusion.1
  14.9 0.1 fusion.33
  15.0 0.0 copy-start.5
  15.0 0.0 copy-start.7
  15.1 15.9 %all-to-all-done = bf16[640,4,128]{0,1,2:T(4,128)(2,1)S(1)} async-done(((bf16[640,4,128]{0,1,2:T(4,128)(2,1)}), bf16[640,4,128]{0,1,2:T(4,128)(2,1)S(1)}, u32[]{:S(2)}, u32[]{:S(2)}) %all-to-all-start) | async-done | bytes 655392 | tf_op jit(solution)/shard_map/all_to_all | solution.py:140
  30.9 0.9 copy.65
  31.9 3.5 %all-to-all-start.1 = ((bf16[640,4,128]{0,2,1:T(8,128)(2,1)}), bf16[640,4,128]{0,2,1:T(8,128)(2,1)S(1)}, u32[]{:S(2)}, u32[]{:S(2)}) async-start(bf16[640,4,128]{0,2,1:T(8,128)(2,1)} %copy.65), calls=%async_computation.1 | async-start | bytes 1310720 | tf_op jit(solution)/shard_map/all_to_all | solution.py:142
  35.3 0.6 compare_convert_fusion
  36.0 0.1 multiply_add_fusion
  36.1 9.4 %all-to-all-done.1 = bf16[640,4,128]{0,2,1:T(8,128)(2,1)S(1)} async-done(((bf16[640,4,128]{0,2,1:T(8,128)(2,1)}), bf16[640,4,128]{0,2,1:T(8,128)(2,1)S(1)}, u32[]{:S(2)}, u32[]{:S(2)}) %all-to-all-start.1) | async-done | bytes 655392 | tf_op jit(solution)/shard_map/all_to_all | solution.py:142
  45.5 0.3 copy.66
  45.9 0.3 rev.8
  46.3 0.0 copy-start.1
  46.3 2.0 %fusion = f32[448,128]{1,0:T(8,128)S(1)} fusion(bf16[1,2,448,1280]{3,2,1,0:T(8,128)(2,1)} %param.13, bf16[1280,128]{1,0:T(8,128)(2,1)S(1)} %rev.8, bf16[1280,128]{1,0:T(8,128)(2,1)S(1)} %bitcast.105, f32[1280]{0:T(1024)S(1)} %broadcast_select_fusion, f32[448]{0:T(512)S(1)} %get-tuple-element.26), kind=kOutput, calls=%fused_computation.5 | convolution fusion | flops 147677184 | bytes 2038528 | tf_op jit(solution)/shard_map/dot_general | solution.py:63
  48.3 0.6 fusion.1
  48.9 0.0 copy-start.2
  48.9 0.2 copy.67
  49.1 0.0 copy-start.8
  49.1 0.0 copy-start.6
  49.1 0.0 copy-start.3
  49.1 0.3 reshape.149
  49.4 0.1 fusion.40
  49.5 0.1 copy-done.2
  49.6 0.2 fusion.11
  49.8 0.2 fusion.9
  50.1 0.2 convolution_bitcast_fusion.1
  50.4 0.2 fusion.13
  50.7 0.1 fusion.41
  50.8 0.1 copy.73
  50.9 0.1 slice.56
  51.0 1.6 %fusion.2 = f32[128,1280]{1,0:T(8,128)S(1)} fusion(bf16[448,128]{0,1:T(8,128)(2,1)S(1)} %slice.56, bf16[1,2,448,1280]{3,2,1,0:T(8,128)(2,1)} %param.13), kind=kOutput, calls=%fused_computation.7 | convolution fusion | flops 146800640 | bytes 1916928 | tf_op jit(solution)/shard_map/dot_general | solution.py:103
  52.7 0.1 copy.72
  52.8 0.1 slice.54
  52.9 1.6 %fusion.5 = f32[128,1280]{1,0:T(8,128)S(1)} fusion(bf16[448,128]{0,1:T(8,128)(2,1)S(1)} %slice.54, bf16[1,2,448,1280]{3,2,1,0:T(8,128)(2,1)} %param.13), kind=kOutput, calls=%fused_computation.10 | convolution fusion | flops 146800640 | bytes 1916928 | tf_op jit(solution)/shard_map/dot_general | solution.py:100
  54.5 0.1 fusion.22
  54.6 0.1 multiply_bitcast_fusion
  54.7 1.0 %rev.9 = bf16[1280,128]{0,1:T(8,128)(2,1)S(1)} reverse(bf16[1280,128]{0,1:T(8,128)(2,1)S(1)} %multiply_bitcast_fusion), dimensions={0} | reverse | bytes 655360 | tf_op jit(solution)/shard_map/jit(_flip)/rev | solution.py:109
  55.8 0.5 broadcast.172
  56.3 1.1 %reduce = bf16[2560,128]{0,1:T(8,128)(2,1)S(1)} reduce(bf16[2560,1,128]{0,2,1:T(8,128)(2,1)S(1)} %pad_maximum_fusion, bf16[]{:T(256)} %broadcast.172), dimensions={1}, to_apply=%copy.74.reduce_sub_computation | reduce | bytes 1310722 | tf_op jit(solution)/shard_map/concatenate | solution.py:109
  57.4 0.3 copy.96
  57.7 0.2 reshape.190
  57.9 12.6 %all_to_all.43 = bf16[4,2,40960]{2,1,0:T(2,128)(2,1)S(1)} all-to-all(bf16[4,2,40960]{2,1,0:T(2,128)(2,1)S(1)} %reshape.190), channel_id=1, replica_groups=mesh['band'=4,'lev'=8] {'band'}, dimensions={0} | all-to-all | bytes 1310720 | tf_op jit(solution)/shard_map/all_to_all | solution.py:160
  70.5 0.6 reshape.191
  71.1 0.1 copy.78
  71.2 1.3 %copy.75 = bf16[640,4,128]{0,1,2:T(4,128)(2,1)} copy(bf16[640,4,128]{2,0,1:T(8,128)(2,1)S(1)} %bitcast.102) | data formatting | bytes 1310720 | tf_op jit(solution)/shard_map/all_to_all | solution.py:160
  72.5 3.6 %all-to-all-start.3 = ((bf16[640,4,128]{0,1,2:T(4,128)(2,1)}), bf16[640,4,128]{0,1,2:T(4,128)(2,1)S(1)}, u32[]{:S(2)}, u32[]{:S(2)}) async-start(bf16[640,4,128]{0,1,2:T(4,128)(2,1)} %copy.75), calls=%async_computation.3 | async-start | bytes 1310720 | tf_op jit(solution)/shard_map/all_to_all | solution.py:159
  76.2 0.1 iota_add_fusion
  76.2 0.1 add.133
  76.4 16.8 %all-to-all-done.3 = bf16[640,4,128]{0,1,2:T(4,128)(2,1)S(1)} async-done(((bf16[640,4,128]{0,1,2:T(4,128)(2,1)}), bf16[640,4,128]{0,1,2:T(4,128)(2,1)S(1)}, u32[]{:S(2)}, u32[]{:S(2)}) %all-to-all-start.3) | async-done | bytes 655392 | tf_op jit(solution)/shard_map/all_to_all | solution.py:159
  93.2 0.1 copy.76
  93.3 0.7 gather_fusion.1
  94.0 0.2 select_bitcast_fusion
  94.1 0.9 copy.77
  (24 shorter events, 0.3 us)
Async XLA Ops:
  0.0 2.3 %copy-start = (bf16[640,8,64]{0,2,1:T(8,128)(2,1)S(1)}, bf16[640,8,64]{0,2,1:T(8,128)(2,1)}, u32[]{:S(2)}) copy-start(bf16[640,8,64]{0,2,1:T(8,128)(2,1)} %param.12) | copy-start | bytes 1966084
  5.3 9.8 %copy-start.4 = (s32[1280]{0:T(1024)S(1)}, s32[1280]{0:T(1024)}, u32[]{:S(2)}) copy-start(s32[1280]{0:T(1024)} %param.15) | copy-start | bytes 15364
  6.4 24.6 %all-to-all-start = ((bf16[640,4,128]{0,1,2:T(4,128)(2,1)}), bf16[640,4,128]{0,1,2:T(4,128)(2,1)S(1)}, u32[]{:S(2)}, u32[]{:S(2)}) async-start(bf16[640,4,128]{0,1,2:T(4,128)(2,1)} %bitcast.2), calls=%async_computation | async-start | bytes 1310720 | tf_op jit(solution)/shard_map/all_to_all | solution.py:140
  15.0 21.0 %copy-start.5 = (f32[1280]{0:T(1024)S(1)}, f32[1280]{0:T(1024)}, u32[]{:S(2)}) copy-start(f32[1280]{0:T(1024)} %param.14) | copy-start | bytes 15364
  15.0 21.0 %copy-start.7 = (f32[16]{0:T(128)S(1)}, f32[16]{0:T(128)}, u32[]{:S(2)}) copy-start(f32[16]{0:T(128)} %param.19) | copy-start | bytes 196
  31.9 13.7 %all-to-all-start.1 = ((bf16[640,4,128]{0,2,1:T(8,128)(2,1)}), bf16[640,4,128]{0,2,1:T(8,128)(2,1)S(1)}, u32[]{:S(2)}, u32[]{:S(2)}) async-start(bf16[640,4,128]{0,2,1:T(8,128)(2,1)} %copy.65), calls=%async_computation.1 | async-start | bytes 1310720 | tf_op jit(solution)/shard_map/all_to_all | solution.py:142
  46.3 2.0 %copy-start.1 = (bf16[1,2,448,1280]{3,2,1,0:T(8,128)(2,1)S(1)}, bf16[1,2,448,1280]{3,2,1,0:T(8,128)(2,1)}, u32[]{:S(2)}) copy-start(bf16[1,2,448,1280]{3,2,1,0:T(8,128)(2,1)} %param.13) | copy-start | bytes 6881284
  48.9 0.7 copy-start.2
  49.1 0.7 copy-start.8
  49.1 1.0 %copy-start.6 = (f32[16,16]{1,0:T(8,128)S(1)}, f32[16,16]{1,0:T(8,128)}, u32[]{:S(2)}) copy-start(f32[16,16]{1,0:T(8,128)} %param.17) | copy-start | bytes 3076
  49.1 1.2 %copy-start.3 = (f32[16,16]{1,0:T(8,128)S(1)}, f32[16,16]{1,0:T(8,128)}, u32[]{:S(2)}) copy-start(f32[16,16]{1,0:T(8,128)} %param.21) | copy-start | bytes 3076
  72.5 20.7 %all-to-all-start.3 = ((bf16[640,4,128]{0,1,2:T(4,128)(2,1)}), bf16[640,4,128]{0,1,2:T(4,128)(2,1)S(1)}, u32[]{:S(2)}, u32[]{:S(2)}) async-start(bf16[640,4,128]{0,1,2:T(4,128)(2,1)} %copy.75), calls=%async_computation.3 | async-start | bytes 1310720 | tf_op jit(solution)/shard_map/all_to_all | solution.py:159
where the time goes:
time: 95.6 us; the launch traced here: 95 us
  waiting for transfers between devices  42.2 us (44%)
  starting transfers between devices  14.4 us (15%)
  local copies, waits for them, and re-layouts  13.4 us (14%)
  blocking collectives  12.6 us (13%)
  matrix products  6.71 us (7%)
  other arithmetic  4.69 us (5%)
  between operations  1.12 us (1%)
    all_to_all x1, waiting for transfers between devices, per_device(): lax.all_to_all(lax.all_to_all(result[:, None, :], 'band', split_axis=0, c...  16.8 us
    all_to_all x1, waiting for transfers between devices, per_device(): lax.all_to_all(ordered, 'lev', split_axis=2, concat_axis=2, tiled=True)  15.9 us
    all_to_all x1, blocking collectives, per_device(): lax.all_to_all(result[:, None, :], 'band', split_axis=0, concat_axis=1, t...  12.6 us
    all_to_all x1, waiting for transfers between devices, per_device(): lax.all_to_all(level_mixed, 'band', split_axis=1, concat_axis=0, tiled=True)  9.43 us
    all_to_all x1, starting transfers between devices, per_device(): lax.all_to_all(ordered, 'lev', split_axis=2, concat_axis=2, tiled=True)  7.28 us
    all_to_all x1, starting transfers between devices, per_device(): lax.all_to_all(lax.all_to_all(result[:, None, :], 'band', split_axis=0, c...  3.63 us
    all_to_all x1, starting transfers between devices, per_device(): lax.all_to_all(level_mixed, 'band', split_axis=1, concat_axis=0, tiled=True)  3.48 us
    gather x1, local copies, waits for them, and re-layouts, per_device(): ordered = jnp.take(azimuthal_coeffs, column_pick, axis=2)  2.54 us
  transfers between devices with their start and end apart: 3, of which 3 were waited for; matrix products, arithmetic and copies ran while one was open for 2% of the time, Pallas kernels for 0%

commit v1 on v0

--- a/solution.py
+++ b/solution.py
@@ -156,12 +156,22 @@
         hydrostatic_matrix,
         thermal_response,
     )
-    returned = lax.all_to_all(
-        lax.all_to_all(result[:, None, :], "band", split_axis=0, concat_axis=1, tiled=True),
-        "lev",
-        split_axis=2,
-        concat_axis=2,
-        tiled=True,
+    returned = jnp.concatenate(
+        lax.all_to_all(
+            jnp.stack(
+                jnp.split(
+                    lax.all_to_all(
+                        result[:, None, :], "band", split_axis=0, concat_axis=1, tiled=True
+                    ),
+                    lax.axis_size("lev"),
+                    axis=2,
+                )
+            ),
+            "lev",
+            0,
+            0,
+        ),
+        axis=2,
     )
     returned = returned.reshape(lat_rows, band_count, lev_count, level_cols, 2)
     returned = jnp.transpose(returned, (0, 3, 1, 2, 4)).reshape(lat_rows, level_cols, last_width)

time: 95.6 us -> 113 us (1.18)
  local copies, waits for them, and re-layouts: 13.4 us -> 32.5 us
  matrix products: 6.71 us -> 5.2 us
    another operation x0 -> x8, local copies, waits for them, and re-layouts: none -> 6.71 us  [per_device(): jnp.stack(jnp.split(lax.all_to_all(result[:, None, :], 'band', split_axis...]
    unnamed x22 -> x33, local copies, waits for them, and re-layouts: 1.36 us -> 5.79 us
    split x0 -> x2, local copies, waits for them, and re-layouts: none -> 4.18 us  [per_device(): jnp.split(lax.all_to_all(result[:, None, :], 'band', split_axis=0, concat...]
    rev x1, local copies, waits for them, and re-layouts: 0.34 us -> 3.2 us  [analyse_wave(): south = jnp.flip(column[half_rows:], axis=0).astype(jnp.float32)]
    dot_general x1, matrix products: 0.58 us -> 2.04 us  [analyse_wave(): jnp.dot(operator_array[1], odd_part, preferred_element_type=jnp.float32)]
    dot_general x1, matrix products: 1.61 us -> 0.34 us  [complete_harmonic(): lax.dot_general(operator_array[1], refreshed[pair_rows:], contract, prefe...]
    dot_general x1, matrix products: 1.61 us -> 0.34 us  [complete_harmonic(): lax.dot_general(operator_array[0], refreshed[:pair_rows], contract, prefe...]
  transfers between devices with their start and end apart: 3 -> 3, of which waited for: 3 -> 3; matrix products, arithmetic and copies ran while one was open for 2% -> 1% of each run, Pallas kernels for 0% -> 0%
where the time goes in v1:
time: 113 us
  waiting for transfers between devices  42.6 us (38%)
  local copies, waits for them, and re-layouts  32.5 us (29%)
  starting transfers between devices  14.4 us (13%)
  blocking collectives  12.6 us (11%)
  matrix products  5.2 us (5%)
  other arithmetic  4.51 us (4%)
    all_to_all x1, waiting for transfers between devices, per_device(): lax.all_to_all(jnp.stack(jnp.split(lax.all_to_all(result[:, None, :], 'ba...  17 us
    all_to_all x1, waiting for transfers between devices, per_device(): lax.all_to_all(ordered, 'lev', split_axis=2, concat_axis=2, tiled=True)  16 us
    all_to_all x1, blocking collectives, per_device(): lax.all_to_all(result[:, None, :], 'band', split_axis=0, concat_axis=1, t...  12.6 us
    all_to_all x1, waiting for transfers between devices, per_device(): lax.all_to_all(level_mixed, 'band', split_axis=1, concat_axis=0, tiled=True)  9.51 us
    all_to_all x1, starting transfers between devices, per_device(): lax.all_to_all(ordered, 'lev', split_axis=2, concat_axis=2, tiled=True)  7.28 us
    another operation x8, local copies, waits for them, and re-layouts, per_device(): jnp.stack(jnp.split(lax.all_to_all(result[:, None, :], 'band', split_axis...  6.71 us
    unnamed x33, local copies, waits for them, and re-layouts  5.79 us
    split x2, local copies, waits for them, and re-layouts, per_device(): jnp.split(lax.all_to_all(result[:, None, :], 'band', split_axis=0, concat...  4.18 us
  transfers between devices with their start and end apart: 3, of which 3 were waited for; matrix products, arithmetic and copies ran while one was open for 1% of the time, Pallas kernels for 0%

profile of v1, /device:TPU:0, one launch (start us, length us, event | category | flops | bytes accessed | tf_op | source)
XLA Modules:
  0.0 112.8 jit_solution(14515721709049119758)
XLA Ops:
  0.0 1.4 %broadcast_multiply_fusion = (s32[32]{0:T(128)S(1)}, s32[32]{0:T(128)S(1)}, s32[]{:T(128)}) fusion(s32[32]{0:T(128)} %param.16, s32[]{:T(128)S(6)} %add.120), kind=kLoop, calls=%fused_computation.92 | loop fusion | flops 223 | bytes 392 | tf_op jit(solution)/shard_map/mul | solution.py:178
  1.4 0.7 scatter_custom_fusion
  2.1 0.1 add.118
  2.3 0.1 add.133
  2.5 2.5 %gather_fusion = bf16[64,640,8]{1,0,2:T(8,128)(2,1)S(1)} fusion(bf16[640,8,64]{0,2,1:T(8,128)(2,1)S(1)} %copy-done, s32[1024]{0:T(1024)S(1)} %get-tuple-element.36), kind=kCustom, calls=%fused_computation.clone | custom fusion | bytes 1310976 | tf_op jit(solution)/shard_map/jit(_take)/gather | solution.py:135
  5.0 0.1 select_bitcast_fusion.1
  5.2 0.2 reshape.147
  5.4 1.1 copy.88
  6.5 7.3 %all-to-all-start = ((bf16[640,4,128]{0,1,2:T(4,128)(2,1)}), bf16[640,4,128]{0,1,2:T(4,128)(2,1)S(1)}, u32[]{:S(2)}, u32[]{:S(2)}) async-start(bf16[640,4,128]{0,1,2:T(4,128)(2,1)} %bitcast.2), calls=%async_computation | async-start | bytes 1310720 | tf_op jit(solution)/shard_map/all_to_all | solution.py:140
  14.4 0.6 multiply_add_fusion.1
  15.1 16.0 %all-to-all-done = bf16[640,4,128]{0,1,2:T(4,128)(2,1)S(1)} async-done(((bf16[640,4,128]{0,1,2:T(4,128)(2,1)}), bf16[640,4,128]{0,1,2:T(4,128)(2,1)S(1)}, u32[]{:S(2)}, u32[]{:S(2)}) %all-to-all-start) | async-done | bytes 655392 | tf_op jit(solution)/shard_map/all_to_all | solution.py:140
  31.1 0.9 copy.89
  32.0 3.5 %all-to-all-start.1 = ((bf16[640,4,128]{0,2,1:T(8,128)(2,1)}), bf16[640,4,128]{0,2,1:T(8,128)(2,1)S(1)}, u32[]{:S(2)}, u32[]{:S(2)}) async-start(bf16[640,4,128]{0,2,1:T(8,128)(2,1)} %copy.89), calls=%async_computation.1 | async-start | bytes 1310720 | tf_op jit(solution)/shard_map/all_to_all | solution.py:142
  35.5 0.6 compare_convert_fusion
  36.2 9.5 %all-to-all-done.1 = bf16[640,4,128]{0,2,1:T(8,128)(2,1)S(1)} async-done(((bf16[640,4,128]{0,2,1:T(8,128)(2,1)}), bf16[640,4,128]{0,2,1:T(8,128)(2,1)S(1)}, u32[]{:S(2)}, u32[]{:S(2)}) %all-to-all-start.1) | async-done | bytes 655392 | tf_op jit(solution)/shard_map/all_to_all | solution.py:142
  45.7 0.3 copy.90
  46.1 3.2 %rev.8 = bf16[1280,128]{1,0:T(8,128)(2,1)} reverse(bf16[1280,128]{1,0:T(8,128)(2,1)S(1)} %bitcast.122), dimensions={0} | reverse | bytes 655360 | tf_op jit(solution)/shard_map/jit(_flip)/rev | solution.py:59
  49.3 2.0 %fusion.1 = f32[448,128]{1,0:T(8,128)S(1)} fusion(bf16[1,2,448,1280]{3,2,1,0:T(8,128)(2,1)} %param.13, bf16[1280,128]{1,0:T(8,128)(2,1)} %rev.8, bf16[1280,128]{1,0:T(8,128)(2,1)S(1)} %bitcast.124, f32[1280]{0:T(1024)S(1)} %broadcast_select_fusion, f32[448]{0:T(512)S(1)} %get-tuple-element.33), kind=kOutput, calls=%fused_computation.6 | convolution fusion | flops 147677184 | bytes 2038528 | tf_op jit(solution)/shard_map/dot_general | solution.py:64
  51.4 1.5 %fusion = f32[448,128]{1,0:T(8,128)S(1)} fusion(bf16[1,2,448,1280]{3,2,1,0:T(8,128)(2,1)S(1)} %copy-done.1, bf16[1280,128]{1,0:T(8,128)(2,1)} %rev.8, bf16[1280,128]{1,0:T(8,128)(2,1)S(1)} %bitcast.125, f32[1280]{0:T(1024)S(1)} %broadcast_select_fusion, f32[448]{0:T(512)S(1)} %get-tuple-element.34), kind=kOutput, calls=%fused_computation.5 | convolution fusion | flops 147677184 | bytes 2041856 | tf_op jit(solution)/shard_map/dot_general | solution.py:63
  53.0 1.0 copy.91
  54.0 1.3 %reshape.149 = f32[896,4,16,2]{0,3,2,1:T(2,128)S(1)} reshape(f32[896,128]{0,1:T(8,128)} %copy.91) | data formatting | bytes 917504 | tf_op jit(solution)/shard_map/reshape | solution.py:88
  55.4 0.2 fusion.11
  55.6 0.2 fusion.9
  55.9 0.2 convolution_bitcast_fusion.1
  56.1 0.2 fusion.13
  56.4 0.1 fusion.42
  56.5 0.1 copy.97
  56.7 0.1 slice.56
  56.8 0.1 copy.96
  57.0 0.1 slice.54
  57.1 0.3 fusion.5
  57.4 0.3 fusion.2
  57.9 1.0 rev.9
  59.0 0.5 broadcast.172
  59.5 1.1 reduce
  60.6 0.3 copy.128
  60.9 0.2 reshape.190
  61.1 12.6 %all_to_all.43 = bf16[4,2,40960]{2,1,0:T(2,128)(2,1)S(1)} all-to-all(bf16[4,2,40960]{2,1,0:T(2,128)(2,1)S(1)} %reshape.190), channel_id=1, replica_groups=mesh['band'=4,'lev'=8] {'band'}, dimensions={0} | all-to-all | bytes 1310720 | tf_op jit(solution)/shard_map/all_to_all | solution.py:163
  73.7 0.6 reshape.191
  74.4 0.1 copy.110
  74.5 2.9 %fusion.39 = (bf16[640,4,16]{2,0,1:T(8,128)(2,1)}, bf16[1,640,4,16]{3,1,2,0:T(8,128)(2,1)}, bf16[1,640,4,16]{3,1,2,0:T(8,128)(2,1)}, bf16[1,640,4,16]{3,1,2,0:T(...) fusion(bf16[640,4,128]{2,0,1:T(8,128)(2,1)S(1)} %bitcast.118), kind=kLoop, calls=%fused_computation.97 | loop fusion | bytes 1310720 | tf_op jit(solution)/shard_map/split | solution.py:162
  77.3 1.3 %copy.99 = bf16[640,4,16]{0,2,1:T(8,128)(2,1)S(1)} copy(bf16[640,4,16]{2,0,1:T(8,128)(2,1)} %get-tuple-element.8) | data formatting | bytes 163840 | tf_op jit(solution)/shard_map/split | solution.py:162
  78.6 1.3 %copy.106 = bf16[1,640,4,16]{1,3,2,0:T(8,128)(2,1)S(1)} copy(bf16[1,640,4,16]{3,1,2,0:T(8,128)(2,1)} %get-tuple-element.9) | data formatting | bytes 163840 | tf_op jit(solution)/shard_map/stack | solution.py:161
  80.0 1.3 %copy.105 = bf16[1,640,4,16]{1,3,2,0:T(8,128)(2,1)S(1)} copy(bf16[1,640,4,16]{3,1,2,0:T(8,128)(2,1)} %get-tuple-element.10) | data formatting | bytes 163840 | tf_op jit(solution)/shard_map/stack | solution.py:161
  81.3 1.9 %copy.104 = bf16[1,640,4,16]{1,3,2,0:T(8,128)(2,1)} copy(bf16[1,640,4,16]{3,1,2,0:T(8,128)(2,1)} %get-tuple-element.11) | data formatting | bytes 163840 | tf_op jit(solution)/shard_map/stack | solution.py:161
  83.2 0.8 copy.103
  84.0 0.2 copy.102
  84.3 0.2 copy.101
  84.5 0.2 copy.100
  84.7 0.7 constant_dynamic-update-slice_fusion.6
  85.4 0.6 constant_dynamic-update-slice_fusion.5
  86.0 0.6 constant_dynamic-update-slice_fusion.4
  86.7 0.6 constant_dynamic-update-slice_fusion.3
  87.3 0.6 constant_dynamic-update-slice_fusion.2
  88.0 0.6 constant_dynamic-update-slice_fusion.1
  88.6 0.6 constant_dynamic-update-slice_fusion
  89.2 0.6 bitcast_dynamic-update-slice_fusion
  89.9 3.6 %all-to-all-start.3 = ((bf16[8,640,4,16]{1,3,2,0:T(8,128)(2,1)}), bf16[8,640,4,16]{1,3,2,0:T(8,128)(2,1)S(1)}, u32[]{:S(2)}, u32[]{:S(2)}) async-start(bf16[8,640,4,16]{1,3,2,0:T(8,128)(2,1)} %bitcast_dynamic-update-slice_fusion), calls=%async_computation.3 | async-start | bytes 1310720 | tf_op jit(solution)/shard_map/all_to_all | solution.py:160
  93.5 17.0 %all-to-all-done.3 = bf16[8,640,4,16]{1,3,2,0:T(8,128)(2,1)S(1)} async-done(((bf16[8,640,4,16]{1,3,2,0:T(8,128)(2,1)}), bf16[8,640,4,16]{1,3,2,0:T(8,128)(2,1)S(1)}, u32[]{:S(2)}, u32[]{:S(2)}) %all-to-all-start.3) | async-done | bytes 655392 | tf_op jit(solution)/shard_map/all_to_all | solution.py:160
  110.6 0.4 copy.107
  110.9 0.1 copy.108
  111.1 0.7 gather_fusion.1
  111.7 0.2 select_bitcast_fusion
  111.9 0.9 copy.109
  (44 shorter events, 0.8 us)
Async XLA Ops:
  0.0 2.5 %copy-start = (bf16[640,8,64]{0,2,1:T(8,128)(2,1)S(1)}, bf16[640,8,64]{0,2,1:T(8,128)(2,1)}, u32[]{:S(2)}) copy-start(bf16[640,8,64]{0,2,1:T(8,128)(2,1)} %param.12) | copy-start | bytes 1966084
  5.4 9.6 %copy-start.6 = (s32[1280]{0:T(1024)S(1)}, s32[1280]{0:T(1024)}, u32[]{:S(2)}) copy-start(s32[1280]{0:T(1024)} %param.15) | copy-start | bytes 15364
  6.5 24.6 %all-to-all-start = ((bf16[640,4,128]{0,1,2:T(4,128)(2,1)}), bf16[640,4,128]{0,1,2:T(4,128)(2,1)S(1)}, u32[]{:S(2)}, u32[]{:S(2)}) async-start(bf16[640,4,128]{0,1,2:T(4,128)(2,1)} %bitcast.2), calls=%async_computation | async-start | bytes 1310720 | tf_op jit(solution)/shard_map/all_to_all | solution.py:140
  15.0 21.0 %copy-start.7 = (f32[1280]{0:T(1024)S(1)}, f32[1280]{0:T(1024)}, u32[]{:S(2)}) copy-start(f32[1280]{0:T(1024)} %param.14) | copy-start | bytes 15364
  15.1 21.1 %copy-start.9 = (f32[16]{0:T(128)S(1)}, f32[16]{0:T(128)}, u32[]{:S(2)}) copy-start(f32[16]{0:T(128)} %param.19) | copy-start | bytes 196
  32.0 13.7 %all-to-all-start.1 = ((bf16[640,4,128]{0,2,1:T(8,128)(2,1)}), bf16[640,4,128]{0,2,1:T(8,128)(2,1)S(1)}, u32[]{:S(2)}, u32[]{:S(2)}) async-start(bf16[640,4,128]{0,2,1:T(8,128)(2,1)} %copy.89), calls=%async_computation.1 | async-start | bytes 1310720 | tf_op jit(solution)/shard_map/all_to_all | solution.py:142
  49.3 2.1 %copy-start.1 = (bf16[1,2,448,1280]{3,2,1,0:T(8,128)(2,1)S(1)}, bf16[1,2,448,1280]{3,2,1,0:T(8,128)(2,1)}, u32[]{:S(2)}) copy-start(bf16[1,2,448,1280]{3,2,1,0:T(8,128)(2,1)} %param.13) | copy-start | bytes 6881284
  53.0 2.4 %copy-start.4 = (f32[16,16]{1,0:T(8,128)S(1)}, f32[16,16]{1,0:T(8,128)}, u32[]{:S(2)}) copy-start(f32[16,16]{1,0:T(8,128)} %param.20) | copy-start | bytes 3076
  54.0 1.7 %copy-start.10 = (f32[16,16]{1,0:T(8,128)S(1)}, f32[16,16]{1,0:T(8,128)}, u32[]{:S(2)}) copy-start(f32[16,16]{1,0:T(8,128)} %param.18) | copy-start | bytes 3076
  54.0 1.9 %copy-start.8 = (f32[16,16]{1,0:T(8,128)S(1)}, f32[16,16]{1,0:T(8,128)}, u32[]{:S(2)}) copy-start(f32[16,16]{1,0:T(8,128)} %param.17) | copy-start | bytes 3076
  54.0 2.2 %copy-start.5 = (f32[16,16]{1,0:T(8,128)S(1)}, f32[16,16]{1,0:T(8,128)}, u32[]{:S(2)}) copy-start(f32[16,16]{1,0:T(8,128)} %param.21) | copy-start | bytes 3076
  84.0 2.6 %copy-start.3 = (bf16[1,640,4,16]{1,3,2,0:T(8,128)(2,1)S(1)}, bf16[1,640,4,16]{1,3,2,0:T(8,128)(2,1)}, u32[]{:S(2)}) copy-start(bf16[1,640,4,16]{1,3,2,0:T(8,128)(2,1)} %copy.103) | copy-start | bytes 245764
  84.0 3.3 %copy-start.2 = (bf16[1,640,4,16]{1,3,2,0:T(8,128)(2,1)S(1)}, bf16[1,640,4,16]{1,3,2,0:T(8,128)(2,1)}, u32[]{:S(2)}) copy-start(bf16[1,640,4,16]{1,3,2,0:T(8,128)(2,1)} %copy.104) | copy-start | bytes 245764
  89.9 20.7 %all-to-all-start.3 = ((bf16[8,640,4,16]{1,3,2,0:T(8,128)(2,1)}), bf16[8,640,4,16]{1,3,2,0:T(8,128)(2,1)S(1)}, u32[]{:S(2)}, u32[]{:S(2)}) async-start(bf16[8,640,4,16]{1,3,2,0:T(8,128)(2,1)} %bitcast_dynamic-update-slice_fusion), calls=%async_computation.3 | async-start | bytes 1310720 | tf_op jit(solution)/shard_map/all_to_all | solution.py:160
